TPU v7x, 32 devices: a whole 2x2x4 slice. The times are simulated.
32 devices in a mesh: dp: 8 (over y, x, core), tensor: 4 (over z).
Axes of the slice: x: 2, y: 2, z: 4, core: 2. Of those that a mesh axis runs over, the one named last changes fastest.
Arguments:
- tokens_in: bfloat16 [32, 577, 1024], P('dp'), may hold values from -6 to 6
- norm1_gain: float32 [1024], replicated, may hold values from 0.5 to 1.5
- norm1_bias: float32 [1024], replicated, may hold values from -3 to 3
- w_qkv: bfloat16 [1024, 3, 16, 64], P(None, None, 'tensor'), may hold values from -0.1875 to 0.1875
- bias_qv: float32 [2, 16, 64], P(None, 'tensor'), may hold values from -3 to 3
- w_out: bfloat16 [16, 64, 1024], P('tensor'), may hold values from -0.75 to 0.75
- bias_out: float32 [1024], replicated, may hold values from -3 to 3
- norm2_gain: float32 [1024], replicated, may hold values from 0.5 to 1.5
- norm2_bias: float32 [1024], replicated, may hold values from -3 to 3
- w_up: bfloat16 [1024, 4096], P(None, 'tensor'), may hold values from -0.1875 to 0.1875
- bias_up: float32 [4096], P('tensor'), may hold values from -3 to 3
- w_down: bfloat16 [4096, 1024], P('tensor'), may hold values from -0.09375 to 0.09375
- bias_down: float32 [1024], replicated, may hold values from -3 to 3
- cotangent: bfloat16 [32, 577, 1024], P('dp'), may hold values from -6 to 6
Outputs:
- block_out: bfloat16 [32, 577, 1024], P('dp')
- grad_input: float32 [32, 577, 1024], P('dp')
- grad_norm1_gain: float32 [1024], replicated
- grad_norm1_bias: float32 [1024], replicated
- grad_w_qkv: float32 [1024, 3, 16, 64], P(None, None, 'tensor')
- grad_bias_qv: float32 [2, 16, 64], P(None, 'tensor')
- grad_w_out: float32 [16, 64, 1024], P('tensor')
- grad_bias_out: float32 [1024], replicated
- grad_norm2_gain: float32 [1024], replicated
- grad_norm2_bias: float32 [1024], replicated
- grad_w_up: float32 [1024, 4096], P(None, 'tensor')
- grad_bias_up: float32 [4096], P('tensor')
- grad_w_down: float32 [4096, 1024], P('tensor')
- grad_bias_down: float32 [1024], replicated
All inputs are finite; a program needn't handle non-finite values.
Results may differ from a plain program's by a relative error of at most 0.024.
Values may be sent and summed in bfloat16 or wider, within the bound.
No kernel may reach another device: no remote copies, remote signals or barrier semaphores. Data moves between devices by JAX's collectives and lax.ppermute only.
A program may use at most 256 MiB of HBM per device.

v0:
```python
import jax
import jax.numpy as jnp
from jax import lax
from jax.sharding import PartitionSpec as P

inv_root2 = 0.7071067811865476
inv_root_2pi = 0.3989422804014327


def layer_norm(values, gain, shift):
    centre = jnp.mean(values, axis=-1, keepdims=True)
    centred = values - centre
    spread = jnp.mean(centred * centred, axis=-1, keepdims=True)
    inv_std = lax.rsqrt(spread + 1e-06)
    whitened = centred * inv_std
    return (whitened, inv_std, whitened * gain + shift)


def norm_back(grad_out, whitened, inv_std, gain):
    grad_white = grad_out * gain
    inner_part = (
        grad_white
        - jnp.mean(grad_white, axis=-1, keepdims=True)
        - whitened * jnp.mean(grad_white * whitened, axis=-1, keepdims=True)
    )
    return (inv_std * inner_part, jnp.sum(grad_out * whitened, axis=0), jnp.sum(grad_out, axis=0))


def gelu(pre_act):
    return 0.5 * pre_act * (1.0 + lax.erf(pre_act * inv_root2))


def gelu_slope(pre_act):
    return 0.5 * (1.0 + lax.erf(pre_act * inv_root2)) + pre_act * inv_root_2pi * jnp.exp(
        -0.5 * pre_act * pre_act
    )


def attend(queries, key_rows, values, score_scale):
    scores = (
        jnp.einsum("qhd,khd->hqk", queries, key_rows, preferred_element_type=jnp.float32)
        * score_scale
    )
    row_max = jnp.max(scores, axis=-1, keepdims=True)
    expos = jnp.exp(scores - row_max)
    expsum = jnp.sum(expos, axis=-1, keepdims=True)
    probs = (expos / expsum).astype(jnp.bfloat16)
    attended = jnp.einsum("hqk,khd->qhd", probs, values, preferred_element_type=jnp.float32).astype(
        jnp.bfloat16
    )
    return (attended, (row_max + jnp.log(expsum))[..., 0])


def attend_back(queries, key_rows, values, upstream, log_norm, score_scale):
    scores = (
        jnp.einsum("qhd,khd->hqk", queries, key_rows, preferred_element_type=jnp.float32)
        * score_scale
    )
    probs = jnp.exp(scores - log_norm[..., None])
    grad_values = jnp.einsum(
        "hqk,qhd->khd", probs.astype(jnp.bfloat16), upstream, preferred_element_type=jnp.float32
    )
    grad_prob = jnp.einsum("qhd,khd->hqk", upstream, values, preferred_element_type=jnp.float32)
    row_delta = jnp.sum(probs * grad_prob, axis=-1, keepdims=True)
    grad_score = (probs * (grad_prob - row_delta) * score_scale).astype(jnp.bfloat16)
    grad_queries = jnp.einsum(
        "hqk,khd->qhd", grad_score, key_rows, preferred_element_type=jnp.float32
    )
    grad_keys = jnp.einsum("hqk,qhd->khd", grad_score, queries, preferred_element_type=jnp.float32)
    return (grad_queries, grad_keys, grad_values)


def body(
    tokens_in,
    norm1_gain,
    norm1_bias,
    w_qkv,
    bias_qv,
    w_out,
    bias_out,
    norm2_gain,
    norm2_bias,
    w_up,
    bias_up,
    w_down,
    bias_down,
    cotangent,
):
    images, seq_len, model_width = tokens_in.shape
    tok_rows = images * seq_len
    heads_local = w_qkv.shape[2]
    head_size = w_qkv.shape[3]
    inner_width = heads_local * head_size
    score_scale = head_size ** (-0.5)
    image_shape = (images, seq_len, heads_local, head_size)
    x_float = tokens_in.reshape(tok_rows, model_width).astype(jnp.float32)
    white1, inv1, normed1 = layer_norm(x_float, norm1_gain, norm1_bias)
    first_in = normed1.astype(jnp.bfloat16)
    w_flat = w_qkv.reshape(model_width, 3 * inner_width)
    projected = jnp.dot(first_in, w_flat, preferred_element_type=jnp.float32).reshape(
        tok_rows, 3, heads_local, head_size
    )
    queries = (projected[:, 0] + bias_qv[0]).astype(jnp.bfloat16).reshape(image_shape)
    key_rows = projected[:, 1].astype(jnp.bfloat16).reshape(image_shape)
    values = (projected[:, 2] + bias_qv[1]).astype(jnp.bfloat16).reshape(image_shape)
    attended, log_norm = lax.map(
        lambda packed: attend(packed[0], packed[1], packed[2], score_scale),
        (queries, key_rows, values),
    )
    head_flat = attended.reshape(tok_rows, inner_width)
    out_rows = w_out.reshape(inner_width, model_width)
    attn_sum = lax.psum(
        jnp.dot(head_flat, out_rows, preferred_element_type=jnp.float32).astype(jnp.bfloat16),
        "tensor",
    ).astype(jnp.float32)
    hidden1 = x_float + attn_sum + bias_out
    white2, inv2, normed2 = layer_norm(hidden1, norm2_gain, norm2_bias)
    second_in = normed2.astype(jnp.bfloat16)
    pre_act = jnp.dot(second_in, w_up, preferred_element_type=jnp.float32) + bias_up
    hidden_act = gelu(pre_act).astype(jnp.bfloat16)
    mlp_sum = lax.psum(
        jnp.dot(hidden_act, w_down, preferred_element_type=jnp.float32).astype(jnp.bfloat16),
        "tensor",
    ).astype(jnp.float32)
    block_out = (hidden1 + mlp_sum + bias_down).astype(jnp.bfloat16)
    grad_out = cotangent.reshape(tok_rows, model_width)
    grad_float = grad_out.astype(jnp.float32)
    grad_bias_down = jnp.sum(grad_float, axis=0)
    grad_w_down = jnp.einsum("rf,re->fe", hidden_act, grad_out, preferred_element_type=jnp.float32)
    grad_hidden = jnp.einsum("re,fe->rf", grad_out, w_down, preferred_element_type=jnp.float32)
    grad_pre = grad_hidden * gelu_slope(pre_act)
    grad_bias_up = jnp.sum(grad_pre, axis=0)
    grad_pre_bf = grad_pre.astype(jnp.bfloat16)
    grad_w_up = jnp.einsum("re,rf->ef", second_in, grad_pre_bf, preferred_element_type=jnp.float32)
    grad_second = lax.psum(
        jnp.einsum("rf,ef->re", grad_pre_bf, w_up, preferred_element_type=jnp.float32).astype(
            jnp.bfloat16
        ),
        "tensor",
    ).astype(jnp.float32)
    grad_norm2_in, grad_norm2_gain, grad_norm2_bias = norm_back(
        grad_second, white2, inv2, norm2_gain
    )
    grad_hidden1 = grad_float + grad_norm2_in
    grad_bias_out = jnp.sum(grad_hidden1, axis=0)
    grad_h1_bf = grad_hidden1.astype(jnp.bfloat16)
    grad_w_out = jnp.einsum(
        "rk,re->ke", head_flat, grad_h1_bf, preferred_element_type=jnp.float32
    ).reshape(heads_local, head_size, model_width)
    upstream = jnp.einsum(
        "re,ke->rk", grad_h1_bf, out_rows, preferred_element_type=jnp.float32
    ).astype(jnp.bfloat16)
    grad_queries, grad_keys, grad_values = lax.map(
        lambda packed: attend_back(
            packed[0], packed[1], packed[2], packed[3], packed[4], score_scale
        ),
        (queries, key_rows, values, upstream.reshape(image_shape), log_norm),
    )
    grad_queries = grad_queries.reshape(tok_rows, heads_local, head_size)
    grad_keys = grad_keys.reshape(tok_rows, heads_local, head_size)
    grad_values = grad_values.reshape(tok_rows, heads_local, head_size)
    grad_bias_qv = jnp.stack([jnp.sum(grad_queries, axis=0), jnp.sum(grad_values, axis=0)])
    grad_qkv = (
        jnp.stack([grad_queries, grad_keys, grad_values], axis=1)
        .astype(jnp.bfloat16)
        .reshape(tok_rows, 3 * inner_width)
    )
    grad_w_qkv = jnp.einsum(
        "re,rk->ek", first_in, grad_qkv, preferred_element_type=jnp.float32
    ).reshape(model_width, 3, heads_local, head_size)
    grad_first = lax.psum(
        jnp.einsum("rk,ek->re", grad_qkv, w_flat, preferred_element_type=jnp.float32).astype(
            jnp.bfloat16
        ),
        "tensor",
    ).astype(jnp.float32)
    grad_norm1_in, grad_norm1_gain, grad_norm1_bias = norm_back(
        grad_first, white1, inv1, norm1_gain
    )
    grad_input = (grad_hidden1 + grad_norm1_in).reshape(images, seq_len, model_width)
    everything = (
        lax.psum(grad_norm1_gain.astype(jnp.bfloat16), "dp").astype(jnp.float32),
        lax.psum(grad_norm1_bias.astype(jnp.bfloat16), "dp").astype(jnp.float32),
        lax.psum(grad_w_qkv.astype(jnp.bfloat16), "dp").astype(jnp.float32),
        lax.psum(grad_bias_qv.astype(jnp.bfloat16), "dp").astype(jnp.float32),
        lax.psum(grad_w_out.astype(jnp.bfloat16), "dp").astype(jnp.float32),
        lax.psum(grad_bias_out.astype(jnp.bfloat16), "dp").astype(jnp.float32),
        lax.psum(grad_norm2_gain.astype(jnp.bfloat16), "dp").astype(jnp.float32),
        lax.psum(grad_norm2_bias.astype(jnp.bfloat16), "dp").astype(jnp.float32),
        lax.psum(grad_w_up.astype(jnp.bfloat16), "dp").astype(jnp.float32),
        lax.psum(grad_bias_up.astype(jnp.bfloat16), "dp").astype(jnp.float32),
        lax.psum(grad_w_down.astype(jnp.bfloat16), "dp").astype(jnp.float32),
        lax.psum(grad_bias_down.astype(jnp.bfloat16), "dp").astype(jnp.float32),
    )
    return (
        block_out.reshape(images, seq_len, model_width),
        grad_input,
        everything[0],
        everything[1],
        everything[2],
        everything[3],
        everything[4],
        everything[5],
        everything[6],
        everything[7],
        everything[8],
        everything[9],
        everything[10],
        everything[11],
    )


def solution(mesh):
    placed = (
        P("dp", None, None),
        P(),
        P(),
        P(None, None, "tensor", None),
        P(None, "tensor", None),
        P("tensor", None, None),
        P(),
        P(),
        P(),
        P(None, "tensor"),
        P("tensor"),
        P("tensor", None),
        P(),
        P("dp", None, None),
    )
    return jax.shard_map(
        body,
        mesh=mesh,
        in_specs=placed,
        out_specs=(
            P("dp", None, None),
            P("dp", None, None),
            P(),
            P(),
            P(None, None, "tensor", None),
            P(None, "tensor", None),
            P("tensor", None, None),
            P(),
            P(),
            P(),
            P(None, "tensor"),
            P("tensor"),
            P("tensor", None),
            P(),
        ),
        check_vma=False,
    )
```

profile of v0, /device:TPU:0, one launch (start us, length us, event | category | flops | bytes accessed | tf_op | source)
XLA Modules:
  0.0 1275.7 jit_solution(7778896030707905259)
XLA Ops:
  7.3 4.4 convert_reduce_fusion
  11.7 3.3 multiply_reduce_fusion.3
  15.9 4.4 add_convert_fusion.2
  20.3 3.8 copy.95
  24.1 5.8 reshape.211
  29.9 6.9 fusion.105
  40.6 3.2 convert_element_type.170
  45.0 4.3 squeeze.33
  49.3 4.3 squeeze.32
  53.5 3.9 fusion.108
  57.4 25.5 %while.26 = (s32[]{:T(128)}, bf16[4,577,4,64]{1,3,2,0:T(8,128)(2,1)}, f32[4,4,577]{2,1,0:T(4,128)S(1)}, bf16[4,577,4,64]{1,3,2,0:T(8,128)(2,1)}, bf16[4,577,4,64...) while((s32[]{:T(128)}, bf16[4,577,4,64]{1,3,2,0:T(8,128)(2,1)}, ...), condition=%wide.region_5.6_spmd, body=%wide.region_2.5_spmd.sunk | while | flops 353050112 | bytes 17370328 | solution.py:106
  82.9 3.9 copy.99
  86.8 3.5 reshape.204
  90.3 5.1 convolution_convert_fusion.2
  95.7 7.7 copy.90
  103.4 6.6 copy.100
  110.0 5.7 reshape.207
  115.7 8.5 reshape.210
  124.2 146.8 %all-reduce.8.cloned.1.call-done = bf16[2308,1024]{1,0:T(8,128)(2,1)} async-done(((bf16[2308,1024]{1,0:T(8,128)(2,1)}), bf16[2308,1024]{1,0:T(8,128)(2,1)}) %all-reduce.8.cloned.1.call-update) | async-done | bytes 4726800 | tf_op jit(solution)/shard_map/psum | solution.py:112
  270.9 9.9 fusion.129
  280.9 5.0 multiply_reduce_fusion.2
  287.3 9.7 multiply_convert_fusion.1
  297.0 11.2 fusion.131
  310.4 6.7 convolution_convert_fusion
  317.3 10.2 convolution_convert_fusion.4
  327.5 8.1 fusion.115
  335.6 153.3 %all-reduce.10.cloned.1.call-done = bf16[2308,1024]{1,0:T(8,128)(2,1)} async-done(((bf16[2308,1024]{1,0:T(8,128)(2,1)}), bf16[2308,1024]{1,0:T(8,128)(2,1)}) %all-reduce.10.cloned.1.call-update) | async-done | bytes 4726800 | tf_op jit(solution)/shard_map/psum | solution.py:135
  489.0 9.1 fusion.91
  498.1 7.6 fusion.127
  514.2 3.2 copy.103
  517.4 198.5 %while.27 = (s32[]{:T(128)}, f32[4,577,4,64]{1,3,2,0:T(8,128)}, bf16[4,577,4,64]{1,0,3,2:T(4,128)(2,1)}, f32[4,577,4,64]{1,3,2,0:T(8,128)}, bf16[4,577,4,64]{1,3...) while((s32[]{:T(128)}, f32[4,577,4,64]{1,3,2,0:T(8,128)}, ...), condition=%wide.region_15.16_spmd, body=%wide.region_13.15_spmd.sunk | while | flops 880270016 | bytes 90938144 | solution.py:153
  524.1 4.7 fusion.178
  528.8 11.9 fusion.181
  540.7 12.2 fusion.180
  554.4 12.7 dynamic_update_slice.31
  573.7 4.7 fusion.178
  578.4 11.9 fusion.181
  590.3 12.2 fusion.180
  604.0 12.7 dynamic_update_slice.31
  623.3 4.7 fusion.178
  628.0 11.9 fusion.181
  639.9 12.2 fusion.180
  653.6 12.7 dynamic_update_slice.31
  672.9 4.7 fusion.178
  677.6 11.9 fusion.181
  689.5 12.2 fusion.180
  703.2 12.7 dynamic_update_slice.31
  718.6 3.4 copy.106
  724.2 3.4 copy.104
  729.4 8.4 fusion.118
  737.9 9.7 convolution_convert_fusion.1
  747.6 5.6 bitcast_convert_fusion
  754.5 4.4 reduce_sum.196
  766.1 74.9 %all-reduce.12.cloned.1.call-done = (bf16[1024,3,4,64]{0,3,2,1:T(8,128)(2,1)}, bf16[4,64,1024]{2,1,0:T(8,128)(2,1)}, bf16[1024,1024]{1,0:T(8,128)(2,1)}, bf16[1024,1024]{1,0:T(8,128)(2,1)}) async-done(((bf16[1024,3,4,64]{0,3,2,1:T(8,128)(2,1)}, bf16[4,64,1024]{2,1,0:T(8,128)(2,1)}, bf16[1024,1024]{1,0:T(8,128)(2,1)}, bf16[1024,1024]{1,0:T(8,128)(2,1)}), (bf16[1024,3,4,64]{0,3,2,1:T(8,128)(2,1)}, ...) | async-done | bytes 6291472 | tf_op jit(solution)/shard_map/psum | solution.py:184
  843.3 3.5 convert_element_type.192
  851.7 318.5 %all-reduce.14.cloned.1.call-done = (bf16[2308,1024]{1,0:T(8,128)(2,1)}, bf16[2308,1024]{1,0:T(8,128)(2,1)}) async-done(((bf16[2308,1024]{1,0:T(8,128)(2,1)}, bf16[2308,1024]{1,0:T(8,128)(2,1)}), (bf16[2308,1024]{1,0:T(8,128)(2,1)}, bf16[2308,1024]{1,0:T(8,128)(2,1)})) %all-reduce.14.cloned.1.call-update) | async-done | bytes 9453584 | tf_op jit(solution)/shard_map/psum | solution.py:121
  1173.4 8.6 fusion.96
  1182.0 23.8 %all-reduce = (bf16[1024]{0:T(1024)(128)(2,1)S(1)}, bf16[1024]{0:T(1024)(128)(2,1)S(1)}, bf16[2,4,64]{2,1,0:T(4,128)(2,1)S(1)}, bf16[1024]{0:T(1024)(128)(2,1)S(...) all-reduce(bf16[1024]{0:T(1024)(128)(2,1)S(1)} %get-tuple-element.2, ...), channel_id=1, replica_groups=mesh['dp'=8,'tensor'=4] {'dp'}, use_global_device_ids=true, to_apply=%region_20.21 | all-reduce | flops 7680 | bytes 30720 | tf_op jit(solution)/shard_map/psum | solution.py:182
  1210.6 9.1 add_convert_fusion
  1219.6 5.8 reshape.206
  1225.4 8.2 copy.107
  1233.6 13.2 %fusion.94 = f32[2308,1024]{1,0:T(8,128)} fusion(f32[2308,1024]{1,0:T(8,128)} %copy-done.4, bf16[2308,1024]{1,0:T(8,128)(2,1)} %get-tuple-element.266, f32[2308,1024]{1,0:T(8,128)} %reshape.210, f32[2308]{0:T(1024)S(1)} %broadcast_multiply_fusion.1, f32[2308]{0:T(1024)S(1)} %div.41, f32[2308]{0:T(1024)S(1)} %broadcast_multiply_fusion.2, ...), kind=kLoop, calls=%fused_computation.84 | loop fusion | flops 21270528 | bytes 33128512 | tf_op jit(solution)/shard_map/add | solution.py:180
  1246.8 8.6 reshape.209
  1255.4 13.5 %copy.108 = f32[4,577,1024]{2,0,1:T(4,128)} copy(f32[4,577,1024]{2,1,0:T(8,128)} %reshape.209) | data formatting | bytes 18907136
  (169 shorter events, 106.5 us)
Async XLA Ops:
  7.2 278.7 %copy-start = (bf16[1024,1024]{1,0:T(8,128)(2,1)S(1)}, bf16[1024,1024]{1,0:T(8,128)(2,1)}, u32[]{:S(2)}) copy-start(bf16[1024,1024]{1,0:T(8,128)(2,1)} %param.27) | copy-start | bytes 6291460
  7.2 8.7 copy-start.19
  7.2 8.7 copy-start.23
  7.2 263.7 %all-reduce.8.cloned.1.call-start = ((), (), s32[]{:S(2)}) async-start(), calls=%async_computation | async-start | bytes 9469952 | tf_op jit(solution)/shard_map/psum | solution.py:112
  7.3 4.4 copy-start.5
  11.7 8.6 copy-start.10
  15.1 0.8 copy-start.12
  36.8 3.8 copy-start.25
  82.9 12.5 copy-start.7
  95.4 393.6 %all-reduce.10.cloned.1.call-start = ((), (), s32[]{:S(2)}) async-start(), calls=%async_computation.1 | async-start | bytes 9469952 | tf_op jit(solution)/shard_map/psum | solution.py:135
  115.7 155.2 %copy-start.24 = (f32[1024]{0:T(1024)S(1)}, f32[1024]{0:T(1024)}, u32[]{:S(2)}) copy-start(f32[1024]{0:T(1024)} %param.24) | copy-start | bytes 12292
  280.9 6.4 copy-start.3
  280.9 6.4 copy-start.21
  280.9 6.4 copy-start.30
  280.9 6.4 copy-start.31
  280.9 16.1 %slice-start.3 = ((s8[4734976]{0:T(1024)(128)(4,1)}), s8[4194304]{0:T(1024)(128)(4,1)S(1)}, s32[]{:S(2)}) async-start(s8[4734976]{0:T(1024)(128)(4,1)} %bitcast.172), calls=%async_computation.7 | async-start | bytes 8388608
  287.3 9.7 slice-start.4
  287.3 9.7 copy-start.28
  308.2 2.2 copy-start.32
  317.2 10.3 slice-start
  317.2 523.8 %all-reduce.12.cloned.1.call-start = ((), (), s32[]{:S(2)}) async-start(), calls=%async_computation.2 | async-start | bytes 12582912 | tf_op jit(solution)/shard_map/psum | solution.py:184
  317.3 10.2 slice-start.1
  317.3 10.2 slice-start.2
  317.3 10.2 copy-start.33
  489.0 9.1 copy-start.6
  498.1 7.6 copy-start.16
  505.6 3.7 copy-start.4
  505.7 3.7 copy-start.9
  511.9 5.6 copy-start.8
  519.6 2.5 copy-start.2
  569.2 2.5 copy-start.2
  618.8 2.5 copy-start.2
  668.4 2.5 copy-start.2
  737.9 9.8 copy-start.17
  737.9 432.4 %all-reduce.14.cloned.1.call-start = ((), (), s32[]{:S(2)}) async-start(), calls=%async_computation.3 | async-start | bytes 18939904 | tf_op jit(solution)/shard_map/psum | solution.py:121
  737.9 9.7 copy-start.18
  737.9 9.7 copy-start.29
  753.2 1.0 copy-start.11
  753.2 1.1 copy-start.13
  841.0 5.8 copy-start.15
  841.0 8.2 copy-start.14
  849.2 324.1 %copy-start.20 = (f32[1024]{0:T(1024)S(1)}, f32[1024]{0:T(1024)}, u32[]{:S(2)}) copy-start(f32[1024]{0:T(1024)} %param.19) | copy-start | bytes 12292
  1173.3 8.6 copy-start.22
  1173.4 8.6 copy-start.27
  1173.4 37.2 %copy-start.26 = (f32[1024]{0:T(1024)S(1)}, f32[1024]{0:T(1024)}, u32[]{:S(2)}) copy-start(f32[1024]{0:T(1024)} %param.30) | copy-start | bytes 12292
  1246.8 22.1 %copy-start.1 = (bf16[1024,1024]{1,0:T(8,128)(2,1)S(1)}, bf16[1024,1024]{1,0:T(8,128)(2,1)}, u32[]{:S(2)}) copy-start(bf16[1024,1024]{1,0:T(8,128)(2,1)} %param.27) | copy-start | bytes 6291460
Sparse Core Ops, SparseCore 0:
  95.5 175.3 all-reduce.7
  317.3 171.6 all-reduce.9
  738.0 102.9 all-reduce.11
  844.0 326.1 all-reduce.13
where the time goes:
time: 1290 us; the launch traced here: 1280 us
  waiting for transfers between devices  694 us (54%)
  matrix products  238 us (18%)
  local copies, waits for them, and re-layouts  192 us (15%)
  other arithmetic  113 us (9%)
  blocking collectives  23.8 us (2%)
  between operations  14.5 us (1%)
    psum x1, waiting for transfers between devices, body(): lax.psum(jnp.dot(hidden_act, w_down, preferred_element_type=jnp.float32)....  319 us
    psum x1, waiting for transfers between devices, body(): lax.psum(jnp.einsum('rf,ef->re', grad_pre_bf, w_up, preferred_element_typ...  153 us
    psum x1, waiting for transfers between devices, body(): lax.psum(jnp.dot(head_flat, out_rows, preferred_element_type=jnp.float32)...  147 us
    psum x1, waiting for transfers between devices, body(): lax.psum(grad_w_qkv.astype(jnp.bfloat16), 'dp').astype(jnp.float32)  74.9 us
    dynamic_update_slice x8, local copies, waits for them, and re-layouts, body(): lax.map(lambda packed: attend_back(packed[0], packed[1], packed[2], packe...  56.6 us
    dot_general x4, matrix products, attend_back(): jnp.einsum('hqk,khd->qhd', grad_score, key_rows, preferred_element_type=j...  48.8 us
    dot_general x4, matrix products, attend_back(): jnp.einsum('hqk,qhd->khd', grad_score, queries, preferred_element_type=jn...  47.7 us
    unnamed x81, local copies, waits for them, and re-layouts  36.1 us
  transfers between devices with their start and end apart: 4, of which 4 were waited for; matrix products, arithmetic and copies ran while one was open for 7% of the time, Pallas kernels for 0%

commit v1 on v0

--- a/solution.py
+++ b/solution.py
@@ -132,11 +132,14 @@
     grad_bias_up = jnp.sum(grad_pre, axis=0)
     grad_pre_bf = grad_pre.astype(jnp.bfloat16)
     grad_w_up = jnp.einsum("re,rf->ef", second_in, grad_pre_bf, preferred_element_type=jnp.float32)
-    grad_second = lax.psum(
-        jnp.einsum("rf,ef->re", grad_pre_bf, w_up, preferred_element_type=jnp.float32).astype(
-            jnp.bfloat16
-        ),
-        "tensor",
+    grad_second = jnp.sum(
+        lax.all_gather(
+            jnp.einsum("rf,ef->re", grad_pre_bf, w_up, preferred_element_type=jnp.float32).astype(
+                jnp.bfloat16
+            ),
+            "tensor",
+        ),
+        axis=0,
     ).astype(jnp.float32)
     grad_norm2_in, grad_norm2_gain, grad_norm2_bias = norm_back(
         grad_second, white2, inv2, norm2_gain

time: 1290 us -> 1450 us (1.12)
  waiting for transfers between devices: 694 us -> 848 us
  other arithmetic: 113 us -> 128 us
    all_gather x0 -> x1, waiting for transfers between devices: none -> 304 us  [body(): lax.all_gather(jnp.einsum('rf,ef->re', grad_pre_bf, w_up, preferred_eleme...]
    psum x1 -> x0, waiting for transfers between devices: 153 us -> none  [body(): lax.psum(jnp.einsum('rf,ef->re', grad_pre_bf, w_up, preferred_element_typ...]
    reduce_sum x2, other arithmetic: 6.22 us -> 21.5 us  [norm_back(): jnp.sum(grad_out, axis=0)]
    unnamed x81 -> x83, local copies, waits for them, and re-layouts: 36.1 us -> 35.8 us
  transfers between devices with their start and end apart: 4 -> 4, of which waited for: 4 -> 4; matrix products, arithmetic and copies ran while one was open for 7% -> 6% of each run, Pallas kernels for 0% -> 0%
where the time goes in v1:
time: 1450 us; the launch traced here: 1440 us
  waiting for transfers between devices  848 us (58%)
  matrix products  237 us (16%)
  local copies, waits for them, and re-layouts  192 us (13%)
  other arithmetic  128 us (9%)
  blocking collectives  24.2 us (2%)
  between operations  14.7 us (1%)
    psum x1, waiting for transfers between devices, body(): lax.psum(jnp.dot(hidden_act, w_down, preferred_element_type=jnp.float32)....  319 us
    all_gather x1, waiting for transfers between devices, body(): lax.all_gather(jnp.einsum('rf,ef->re', grad_pre_bf, w_up, preferred_eleme...  304 us
    psum x1, waiting for transfers between devices, body(): lax.psum(jnp.dot(head_flat, out_rows, preferred_element_type=jnp.float32)...  147 us
    psum x1, waiting for transfers between devices, body(): lax.psum(grad_w_qkv.astype(jnp.bfloat16), 'dp').astype(jnp.float32)  78 us
    dynamic_update_slice x8, local copies, waits for them, and re-layouts, body(): lax.map(lambda packed: attend_back(packed[0], packed[1], packed[2], packe...  56.6 us
    dot_general x4, matrix products, attend_back(): jnp.einsum('hqk,khd->qhd', grad_score, key_rows, preferred_element_type=j...  48.1 us
    dot_general x4, matrix products, attend_back(): jnp.einsum('hqk,qhd->khd', grad_score, queries, preferred_element_type=jn...  47.1 us
    unnamed x83, local copies, waits for them, and re-layouts  35.8 us
  transfers between devices with their start and end apart: 4, of which 4 were waited for; matrix products, arithmetic and copies ran while one was open for 6% of the time, Pallas kernels for 0%

profile of v1, /device:TPU:0, one launch (start us, length us, event | category | flops | bytes accessed | tf_op | source)
XLA Modules:
  0.0 1444.7 jit_solution(14087641368007954065)
XLA Ops:
  7.3 4.4 convert_reduce_fusion
  11.7 3.3 multiply_reduce_fusion.3
  15.8 4.5 add_convert_fusion.2
  20.3 3.8 copy.95
  24.1 5.7 reshape.215
  29.8 6.9 fusion.106
  45.0 4.3 squeeze.33
  49.2 4.3 squeeze.32
  53.5 3.9 fusion.109
  57.4 25.5 %while.26 = (s32[]{:T(128)}, bf16[4,577,4,64]{1,3,2,0:T(8,128)(2,1)}, f32[4,4,577]{2,1,0:T(4,128)S(1)}, bf16[4,577,4,64]{1,3,2,0:T(8,128)(2,1)}, bf16[4,577,4,64...) while((s32[]{:T(128)}, bf16[4,577,4,64]{1,3,2,0:T(8,128)(2,1)}, ...), condition=%wide.region_5.6_spmd, body=%wide.region_2.5_spmd.sunk | while | flops 353050112 | bytes 17370328 | solution.py:106
  82.9 3.9 copy.99
  86.8 3.5 reshape.204
  90.3 5.1 convolution_convert_fusion.2
  95.8 7.7 copy.90
  103.5 6.6 copy.100
  110.0 5.7 reshape.207
  115.7 8.5 reshape.210
  124.2 146.7 %all-reduce.7.cloned.1.call-done = bf16[2308,1024]{1,0:T(8,128)(2,1)} async-done(((bf16[2308,1024]{1,0:T(8,128)(2,1)}), bf16[2308,1024]{1,0:T(8,128)(2,1)}) %all-reduce.7.cloned.1.call-update) | async-done | bytes 4726800 | tf_op jit(solution)/shard_map/psum | solution.py:112
  271.0 10.0 fusion.131
  281.0 5.0 multiply_reduce_fusion.2
  287.4 9.8 multiply_convert_fusion.1
  297.2 11.2 fusion.133
  310.6 6.7 fusion.101
  317.4 10.2 convolution_convert_fusion.4
  327.7 8.1 fusion.116
  335.8 304.3 %all-gather.4.cloned.1.call-done = bf16[4,2308,1024]{2,1,0:T(8,128)(2,1)} async-done(((bf16[1,2308,1024]{2,1,0:T(8,128)(2,1)}), bf16[4,2308,1024]{2,1,0:T(8,128)(2,1)}) %all-gather.4.cloned.1.call-update) | async-done | bytes 18907152 | tf_op jit(solution)/shard_map/all_gather | solution.py:136
  640.1 18.4 %fusion.128 = (bf16[1024]{0:T(1024)(128)(2,1)}, bf16[2308,1024]{1,0:T(8,128)(2,1)}) fusion(bf16[4,2308,1024]{2,1,0:T(8,128)(2,1)} %all-gather.4.cloned.1.call-done), kind=kLoop, calls=%fused_computation.144 | loop fusion | flops 16542720 | bytes 23635968 | tf_op jit(solution)/shard_map/reduce_sum | solution.py:26
  658.5 9.3 fusion.91
  667.8 7.3 fusion.129
  683.6 3.2 copy.103
  686.8 198.0 %while.27 = (s32[]{:T(128)}, f32[4,577,4,64]{1,3,2,0:T(8,128)}, bf16[4,577,4,64]{1,0,3,2:T(4,128)(2,1)}, f32[4,577,4,64]{1,3,2,0:T(8,128)}, bf16[4,577,4,64]{1,3...) while((s32[]{:T(128)}, f32[4,577,4,64]{1,3,2,0:T(8,128)}, ...), condition=%wide.region_15.16_spmd, body=%wide.region_13.15_spmd.sunk | while | flops 880270016 | bytes 90938144 | solution.py:156
  694.0 4.7 fusion.180
  698.7 11.8 fusion.183
  710.5 12.0 fusion.182
  724.0 12.7 dynamic_update_slice.31
  743.4 4.7 fusion.180
  748.1 11.8 fusion.183
  759.9 12.0 fusion.182
  773.4 12.7 dynamic_update_slice.31
  792.7 4.7 fusion.180
  797.4 11.8 fusion.183
  809.2 12.0 fusion.182
  822.7 12.7 dynamic_update_slice.31
  842.1 4.7 fusion.180
  846.8 11.8 fusion.183
  858.6 12.0 fusion.182
  872.1 12.7 dynamic_update_slice.31
  887.5 3.4 copy.106
  892.9 3.4 copy.104
  898.1 8.4 fusion.119
  906.7 9.5 convolution_convert_fusion.1
  916.2 5.7 bitcast_convert_fusion
  923.1 4.4 reduce_sum.209
  931.6 78.0 %all-reduce.9.cloned.1.call-done = (bf16[1024,3,4,64]{0,3,2,1:T(8,128)(2,1)}, bf16[4,64,1024]{2,1,0:T(8,128)(2,1)}, bf16[1024,1024]{1,0:T(8,128)(2,1)}, bf16[1024,1024]{1,0:T(8,128)(2,1)}) async-done(((bf16[1024,3,4,64]{0,3,2,1:T(8,128)(2,1)}, bf16[4,64,1024]{2,1,0:T(8,128)(2,1)}, bf16[1024,1024]{1,0:T(8,128)(2,1)}, bf16[1024,1024]{1,0:T(8,128)(2,1)}), (bf16[1024,3,4,64]{0,3,2,1:T(8,128)(2,1)}, ...) | async-done | bytes 6291472 | tf_op jit(solution)/shard_map/psum | solution.py:187
  1011.9 3.5 convert_element_type.194
  1020.3 318.5 %all-reduce.11.cloned.1.call-done = (bf16[2308,1024]{1,0:T(8,128)(2,1)}, bf16[2308,1024]{1,0:T(8,128)(2,1)}) async-done(((bf16[2308,1024]{1,0:T(8,128)(2,1)}, bf16[2308,1024]{1,0:T(8,128)(2,1)}), (bf16[2308,1024]{1,0:T(8,128)(2,1)}, bf16[2308,1024]{1,0:T(8,128)(2,1)})) %all-reduce.11.cloned.1.call-update) | async-done | bytes 9453584 | tf_op jit(solution)/shard_map/psum | solution.py:121
  1342.0 8.4 fusion.96
  1350.4 24.2 %all-reduce = (bf16[1024]{0:T(1024)(128)(2,1)S(1)}, bf16[1024]{0:T(1024)(128)(2,1)S(1)}, bf16[2,4,64]{2,1,0:T(4,128)(2,1)S(1)}, bf16[1024]{0:T(1024)(128)(2,1)S(...) all-reduce(bf16[1024]{0:T(1024)(128)(2,1)S(1)} %get-tuple-element.2, ...), channel_id=1, replica_groups=mesh['dp'=8,'tensor'=4] {'dp'}, use_global_device_ids=true, to_apply=%region_20.21 | all-reduce | flops 7680 | bytes 30720 | tf_op jit(solution)/shard_map/psum | solution.py:185
  1379.3 9.0 add_convert_fusion
  1388.3 5.8 reshape.206
  1394.1 8.2 copy.107
  1402.3 13.3 fusion.94
  1415.6 8.6 reshape.209
  1424.2 13.5 copy.108
  (171 shorter events, 106.4 us)
Async XLA Ops:
  7.2 278.8 %copy-start = (bf16[1024,1024]{1,0:T(8,128)(2,1)S(1)}, bf16[1024,1024]{1,0:T(8,128)(2,1)}, u32[]{:S(2)}) copy-start(bf16[1024,1024]{1,0:T(8,128)(2,1)} %param.27) | copy-start | bytes 6291460
  7.2 8.6 copy-start.19
  7.2 8.6 copy-start.24
  7.2 263.8 %all-reduce.7.cloned.1.call-start = ((), (), s32[]{:S(2)}) async-start(), calls=%async_computation | async-start | bytes 9469952 | tf_op jit(solution)/shard_map/psum | solution.py:112
  7.3 4.4 copy-start.5
  11.7 8.5 copy-start.10
  15.1 0.7 copy-start.12
  36.7 3.8 copy-start.26
  82.9 12.5 copy-start.7
  95.4 544.7 %all-gather.4.cloned.1.call-start = ((), (), s32[]{:S(2)}) async-start(), calls=%async_computation.1 | async-start | bytes 23674880 | tf_op jit(solution)/shard_map/all_gather | solution.py:136
  115.7 155.2 %copy-start.25 = (f32[1024]{0:T(1024)S(1)}, f32[1024]{0:T(1024)}, u32[]{:S(2)}) copy-start(f32[1024]{0:T(1024)} %param.24) | copy-start | bytes 12292
  281.0 6.4 copy-start.3
  281.0 6.4 copy-start.21
  281.0 6.4 copy-start.31
  281.0 6.4 copy-start.32
  281.0 16.2 %slice-start.3 = ((s8[4734976]{0:T(1024)(128)(4,1)}), s8[4194304]{0:T(1024)(128)(4,1)S(1)}, s32[]{:S(2)}) async-start(s8[4734976]{0:T(1024)(128)(4,1)} %bitcast.174), calls=%async_computation.7 | async-start | bytes 8388608
  287.4 9.8 slice-start.4
  287.4 9.8 copy-start.29
  308.5 2.1 copy-start.33
  317.3 10.4 slice-start
  317.3 692.3 %all-reduce.9.cloned.1.call-start = ((), (), s32[]{:S(2)}) async-start(), calls=%async_computation.2 | async-start | bytes 12582912 | tf_op jit(solution)/shard_map/psum | solution.py:187
  317.4 10.2 slice-start.1
  317.4 10.2 slice-start.2
  317.4 10.2 copy-start.34
  658.5 9.3 copy-start.6
  667.8 7.4 copy-start.16
  675.1 3.6 copy-start.4
  675.1 3.6 copy-start.9
  681.2 5.6 copy-start.8
  689.4 2.6 copy-start.2
  738.8 2.6 copy-start.2
  788.2 2.6 copy-start.2
  837.5 2.6 copy-start.2
  906.6 9.6 copy-start.17
  906.6 432.3 %all-reduce.11.cloned.1.call-start = ((), (), s32[]{:S(2)}) async-start(), calls=%async_computation.3 | async-start | bytes 18939904 | tf_op jit(solution)/shard_map/psum | solution.py:121
  906.6 9.5 copy-start.18
  906.7 9.5 copy-start.30
  921.9 1.0 copy-start.11
  921.9 1.1 copy-start.13
  1009.6 5.8 copy-start.15
  1009.6 8.2 copy-start.14
  1017.8 324.1 %copy-start.20 = (f32[1024]{0:T(1024)S(1)}, f32[1024]{0:T(1024)}, u32[]{:S(2)}) copy-start(f32[1024]{0:T(1024)} %param.19) | copy-start | bytes 12292
  1342.0 8.4 copy-start.22
  1342.0 8.4 copy-start.23
  1342.0 8.4 copy-start.28
  1342.0 37.4 %copy-start.27 = (f32[1024]{0:T(1024)S(1)}, f32[1024]{0:T(1024)}, u32[]{:S(2)}) copy-start(f32[1024]{0:T(1024)} %param.30) | copy-start | bytes 12292
  1415.6 22.1 %copy-start.1 = (bf16[1024,1024]{1,0:T(8,128)(2,1)S(1)}, bf16[1024,1024]{1,0:T(8,128)(2,1)}, u32[]{:S(2)}) copy-start(bf16[1024,1024]{1,0:T(8,128)(2,1)} %param.27) | copy-start | bytes 6291460
Sparse Core Ops, SparseCore 0:
  95.5 175.3 all-reduce.6
  317.5 322.5 all-gather.3
  906.7 102.8 all-reduce.8
  1012.6 326.1 all-reduce.10
